TPU v7x, 32 devices: a whole 2x2x4 slice. The times are simulated.
32 devices in a mesh: strip: 8 (over z, core), basis: 4 (over y, x).
Axes of the slice: x: 2, y: 2, z: 4, core: 2. Of those that a mesh axis runs over, the one named last changes fastest.
Arguments:
- sky_image: float32 [1024, 1024], P('strip', 'basis'), may hold values from -6 to 6
- dual_coeffs: float32 [8, 1024, 1024], P('basis', 'strip'), may hold values from -2 to 2
- thresholds: float32 [8, 1024, 1024], P('basis', 'strip'), may hold values from 0.05 to 1
Outputs:
- dual_next: float32 [8, 1024, 1024], P('basis', 'strip')
- adjoint_image: float32 [1024, 1024], P('strip', 'basis')
All inputs are finite; a program needn't handle non-finite values.
Results may differ from a plain program's by a relative error of at most 0.00002.
Values sent between devices are 32-bit elements; how exact they have to be, the bound alone decides.
A program may use at most 64 MiB of HBM per device.

v0:
```python
import functools
import math

import jax
import jax.numpy as jnp
import numpy as np
from jax import lax
from jax.experimental import pallas as pl
from jax.experimental.pallas import tpu as pltpu
from jax.sharding import PartitionSpec as P

BASES = 8
LEVELS = 3


daubechies = [
    [0.7071067811865476, 0.7071067811865476],
    [0.48296291314469025, 0.836516303737469, 0.22414386804185735, -0.12940952255092145],
    [
        0.3326705529509569,
        0.8068915093133388,
        0.4598775021193313,
        -0.13501102001039084,
        -0.08544127388224149,
        0.035226291882100656,
    ],
    [
        0.23037781330885523,
        0.7148465705525415,
        0.6308807679295904,
        -0.02798376941698385,
        -0.18703481171888114,
        0.030841381835986965,
        0.032883011666982945,
        -0.010597401784997278,
    ],
    [
        0.160102397974125,
        0.6038292697974729,
        0.7243085284385744,
        0.13842814590110342,
        -0.24229488706619015,
        -0.03224486958502952,
        0.07757149384006515,
        -0.006241490213011705,
        -0.012580751999015526,
        0.003335725285001549,
    ],
    [
        0.11154074335008017,
        0.4946238903983854,
        0.7511339080215775,
        0.3152503517092432,
        -0.22626469396516913,
        -0.12976686756709563,
        0.09750160558707936,
        0.02752286553001629,
        -0.031582039318031156,
        0.0005538422009938016,
        0.004777257511010651,
        -0.00107730108499558,
    ],
    [
        0.07785205408506236,
        0.39653931948230575,
        0.7291320908465551,
        0.4697822874053586,
        -0.14390600392910627,
        -0.22403618499416572,
        0.07130921926705004,
        0.08061260915106681,
        -0.03802993693503463,
        -0.01657454163101562,
        0.012550998556013784,
        0.00042957797300470274,
        -0.0018016407039998328,
        0.0003537138000010399,
    ],
    [
        0.05441584224308161,
        0.3128715909144659,
        0.6756307362980128,
        0.5853546836548691,
        -0.015829105256023893,
        -0.2840155429624281,
        0.00047248457399797254,
        0.128747426620186,
        -0.01736930100202211,
        -0.04408825393106472,
        0.013981027917015516,
        0.008746094047015655,
        -0.00487035299301066,
        -0.0003917403729959771,
        0.0006754494059985568,
        -0.00011747678400228192,
    ],
]


def filter_table():
    low_rows = np.zeros((8, 16), np.float32)
    high_rows = np.zeros((8, 16), np.float32)
    for basis_row, filter_taps in enumerate(daubechies):
        length = len(filter_taps)
        for tap_index in range(length):
            low_rows[basis_row, tap_index] = filter_taps[tap_index]
            high_rows[basis_row, tap_index] = (-1) ** tap_index * filter_taps[
                length - 1 - tap_index
            ]
    return (low_rows, high_rows)


def spread(taps, step):
    wide = np.zeros(((len(taps) - 1) * step + 1,), np.float64)
    wide[::step] = taps
    return wide


def level_table(tile):
    low_rows, high_rows = filter_table()
    table = np.zeros((low_rows.shape[0], 2 * tile, 2 * tile), np.float64)
    for basis in range(low_rows.shape[0]):
        count = 2 * (basis + 1)
        low = low_rows[basis, :count].astype(np.float64)
        high = high_rows[basis, :count].astype(np.float64)
        before, offset = np.ones((1,), np.float64), 0
        for level in range(LEVELS):
            step = 2**level
            low_comp = np.convolve(spread(low, step), before)
            high_comp = np.convolve(spread(high, step), before)
            for row in range(tile // step):
                start = (row // 2) * 2 * step
                comp = low_comp if row % 2 == 0 else high_comp
                table[basis, offset + row, start : start + len(comp)] = comp
            before, offset = low_comp, offset + tile // step
    halves = np.stack([table[:, :, :tile], table[:, :, tile:]], axis=1)
    return halves.astype(np.float32)


def bf16_pair(value):
    high = value.astype(jnp.bfloat16)
    return high, (value - high.astype(jnp.float32)).astype(jnp.bfloat16)


def dot(left, right):
    return lax.dot_general(
        left, right, (((1,), (0,)), ((), ())), preferred_element_type=jnp.float32
    )


def flip_bits(index, mask):
    flipped, bit = index, 1
    while bit <= mask:
        if mask & bit:
            flipped = flipped + bit - 2 * bit * ((index // bit) % 2)
        bit *= 2
    return flipped


def kernel(
    cfg, sky, table, dual, thresholds, out_dual, out_image,
    xg, tabv, wov, a_lhs, a_t, g_an, g_sy, dualv, thrv, z_hi, z_lo, coef, dtile, e_hi, e_lo,
    pbuf, hbuf, rbuf,
    load_sem, store_sem, bs_send, bs_recv, hs_send, hs_recv, rs_send, rs_recv, ps_send, ps_recv,
):
    n_strip, n_basis, bases, tile, width, cols, halo = cfg
    tiles, per_block = cols // tile, width // tile
    strip, me = lax.axis_index("strip"), lax.axis_index("basis")
    after, behind = lax.rem(strip + 1, n_strip), lax.rem(strip + n_strip - 1, n_strip)
    peers = [me] + [flip_bits(me, mask) for mask in range(1, n_basis)]
    norm_scale = 1.0 / math.sqrt(BASES)
    offsets = [0]
    for level in range(LEVELS):
        offsets.append(offsets[-1] + tile // 2**level)
    used = offsets[-1]

    loads = []
    table_copy = pltpu.make_async_copy(table.at[pl.ds(me * bases, bases)], tabv, load_sem.at[0])
    table_copy.start()
    for which, (src, dst) in enumerate(((dual, dualv), (thresholds, thrv))):
        for j in range(tiles):
            copy = pltpu.make_async_copy(
                src.at[:, :, pl.ds(j * tile, tile)], dst.at[:, j], load_sem.at[1 + which * tiles + j]
            )
            copy.start()
            loads.append(copy)

    barrier = pltpu.get_barrier_semaphore()
    for peer in peers[1:]:
        pl.semaphore_signal(barrier, inc=1, device_id=(strip, peer), device_id_type=pl.DeviceIdType.MESH)
    for other in (after, behind):
        pl.semaphore_signal(barrier, inc=1, device_id=(other, me), device_id_type=pl.DeviceIdType.MESH)
    pl.semaphore_wait(barrier, n_basis + 1)

    def remote(src, dst, send, recv, target):
        return pltpu.make_async_remote_copy(
            src_ref=src, dst_ref=dst, send_sem=send, recv_sem=recv,
            device_id=target, device_id_type=pl.DeviceIdType.MESH,
        )

    block_copies = [None]
    for d in range(1, n_basis):
        block_copies.append(
            remote(sky, xg.at[me, pl.ds(0, tile)], bs_send.at[d], bs_recv.at[d], (strip, peers[d]))
        )
    halo_copies = [
        remote(sky.at[pl.ds(0, halo)], xg.at[me, pl.ds(tile, halo)], hs_send.at[0], hs_recv.at[0], (behind, me))
    ]
    for d in range(1, n_basis):
        halo_copies.append(
            remote(
                xg.at[peers[d], pl.ds(0, halo)], xg.at[peers[d], pl.ds(tile, halo)],
                hs_send.at[d], hs_recv.at[d], (behind, me),
            )
        )
    halo_copies[0].start()
    for d in range(1, n_basis):
        block_copies[d].start()

    xg[me, 0:tile, :] = sky[...]
    if halo < tile:
        for d in range(n_basis):
            xg[d, tile + halo :, :] = jnp.zeros((tile - halo, width), jnp.float32)

    table_copy.wait()
    for b in range(bases):
        wov[...] = jnp.zeros_like(wov)
        for half in range(2):
            a_high, a_low = bf16_pair(tabv[b, half, :used])
            a_lhs[b, :used, half * tile : (half + 1) * tile] = a_high
            a_lhs[b, used:, half * tile : (half + 1) * tile] = a_low
            t_high, t_low = bf16_pair(tabv[b, half].T)
            a_t[half * tile : (half + 1) * tile, b * 2 * tile : (b + 1) * 2 * tile] = t_high
            a_t[(2 + half) * tile : (3 + half) * tile, b * 2 * tile : (b + 1) * 2 * tile] = t_low
            for level in range(LEVELS):
                rows = tabv[b, half, offsets[level] : offsets[level + 1]]
                if level > 0:
                    slot = wov.at[level - 1, half]
                    slot[pl.ds(0, tile // 2**level, stride=2**level), :] = rows
                    rows = slot[...]
                g_high, g_low = bf16_pair(rows)
                s = (1 - half) * tile
                g_sy[b, level, s : s + tile, :tile] = g_high
                g_sy[b, level, s : s + tile, tile:] = g_low
                g_high, g_low = bf16_pair(rows.T)
                s = half * tile
                g_an[b, level, s : s + tile, :tile] = g_high
                g_an[b, level, s : s + tile, tile:] = g_low

    for d in range(1, n_basis):
        block_copies[d].wait_recv()
        halo_copies[d].start()

    for d in range(n_basis):
        halo_copies[d].wait_recv()
        x_high, x_low = bf16_pair(xg[peers[d]])
        for b in range(bases):
            wide = dot(a_lhs[b], x_high)
            z = wide[:used] + wide[used:] + dot(a_lhs[b, :used], x_low)
            high, low = bf16_pair(z)
            for part in range(per_block):
                at = peers[d] * per_block + part
                z_hi[b, at, :, :] = high[:, part * tile : (part + 1) * tile]
                z_lo[b, at, :, :] = low[:, part * tile : (part + 1) * tile]

    for copy in loads:
        copy.wait()
    lane = lax.broadcasted_iota(jnp.int32, (tile, tile), 1)
    row = lax.broadcasted_iota(jnp.int32, (tile, tile), 0)
    stores = []

    def windows(source, first, last, step):
        pieces = [source(j)[first:last] for j in range(tiles)]
        return jnp.concatenate(
            [
                jnp.concatenate(
                    [pieces[j], pieces[(j + 1) % tiles]] if step > 0 else [pieces[j - 1], pieces[j]], axis=1
                )
                for j in range(tiles)
            ],
            axis=0,
        )

    def columns(high_src, low_src, matrix, first, last, step):
        wide = dot(windows(high_src, first, last, step), matrix[...])
        return wide[:, :tile] + wide[:, tile:] + dot(windows(low_src, first, last, step), matrix[:, :tile])

    for b in range(bases):
        for level in range(LEVELS):
            y = columns(
                lambda j: z_hi[b, j], lambda j: z_lo[b, j], g_an.at[b, level],
                offsets[level], offsets[level + 1], 1,
            )
            stride, many = 2**level, tile // 2**level
            for j in range(tiles):
                mine = y[j * many : (j + 1) * many]
                slot = coef.at[j]
                if level == 0:
                    slot[...] = mine
                else:
                    held = slot[pl.ds(0, many, stride=stride), :]
                    slot[pl.ds(0, many, stride=stride), :] = jnp.where(
                        lane[:many] % stride == 0, mine, held
                    )
        for j in range(tiles):
            limit = thrv[b, j]
            dtile[b, j, :, :] = jnp.clip(dualv[b, j] + coef[j] * norm_scale, -limit, limit)
            copy = pltpu.make_async_copy(
                dtile.at[b, j], out_dual.at[b, :, pl.ds(j * tile, tile)], store_sem.at[b * tiles + j]
            )
            copy.start()
            stores.append(copy)
        for level in range(LEVELS):
            stride, many = 2**level, tile // 2**level
            highs, lows = [], []
            for j in range(tiles):
                slot = dtile.at[b, j]
                value = slot[...] if level == 0 else slot[pl.ds(0, many, stride=stride), :]
                if level < LEVELS - 1:
                    deeper = (row[:many] % 2 == 0) & (lane[:many] % (2 * stride) == 0)
                    value = jnp.where(deeper, 0.0, value)
                high, low = bf16_pair(value)
                highs.append(high)
                lows.append(low)
            e = columns(lambda j: highs[j], lambda j: lows[j], g_sy.at[b, level], 0, many, -1)
            e_high, e_low = bf16_pair(e)
            first = b * 2 * tile + offsets[level]
            for j in range(tiles):
                e_hi[j, first : first + many, :] = e_high[j * many : (j + 1) * many]
                e_lo[j, first : first + many, :] = e_low[j * many : (j + 1) * many]
        first = b * 2 * tile + used
        rest = 2 * tile - used
        for j in range(tiles):
            e_hi[j, first : first + rest, :] = jnp.zeros((rest, tile), jnp.bfloat16)
            e_lo[j, first : first + rest, :] = jnp.zeros((rest, tile), jnp.bfloat16)

    order = list(range(n_basis - 1, -1, -1))
    carry_copies, part_copies = {}, {}
    for d in order:
        at = peers[d]
        e_h = jnp.concatenate([e_hi[at * per_block + part] for part in range(per_block)], axis=1)
        e_l = jnp.concatenate([e_lo[at * per_block + part] for part in range(per_block)], axis=1)
        wide = dot(a_t[...], e_h)
        pbuf[d, :, :] = wide[: 2 * tile] + wide[2 * tile :] + dot(a_t[: 2 * tile], e_l)
        carry_copies[d] = remote(
            pbuf.at[d, pl.ds(tile, halo)], hbuf.at[d], ps_send.at[d], ps_recv.at[d], (after, me)
        )
        carry_copies[d].start()
    for d in order:
        carry_copies[d].wait_recv()
        pbuf[d, :halo, :] = pbuf[d, :halo, :] + hbuf[d]
        if d > 0:
            part_copies[d] = remote(
                pbuf.at[d, pl.ds(0, tile)], rbuf.at[d], rs_send.at[d], rs_recv.at[d], (strip, peers[d])
            )
            part_copies[d].start()
    total = pbuf[0, :tile, :]
    for d in order:
        if d > 0:
            part_copies[d].wait_recv()
            total = total + rbuf[d]
    out_image[...] = total * norm_scale

    for d in range(n_basis):
        halo_copies[d].wait_send()
        carry_copies[d].wait_send()
        if d > 0:
            block_copies[d].wait_send()
            part_copies[d].wait_send()
    for copy in stores:
        copy.wait()


def solution(mesh):
    n_strip, n_basis = mesh.shape["strip"], mesh.shape["basis"]

    def on_device(sky_image, dual_coeffs, thresholds):
        bases, tile, cols = dual_coeffs.shape
        width = sky_image.shape[1]
        tiles = cols // tile
        reach = 2 * BASES - 2
        halo = -(-reach * (2**LEVELS - 1) // 8) * 8
        assert halo <= tile and width % tile == 0 and cols == width * n_basis
        assert n_basis & (n_basis - 1) == 0 and tile % 2**LEVELS == 0
        used = sum(tile // 2**level for level in range(LEVELS))
        f32, bf16 = jnp.float32, jnp.bfloat16
        dma = pltpu.SemaphoreType.DMA
        vmem, anywhere = pl.BlockSpec(memory_space=pltpu.VMEM), pl.BlockSpec(memory_space=pl.ANY)
        table = jnp.asarray(level_table(tile))
        return pl.pallas_call(
            functools.partial(kernel, (n_strip, n_basis, bases, tile, width, cols, halo)),
            out_shape=(
                jax.ShapeDtypeStruct(dual_coeffs.shape, f32),
                jax.ShapeDtypeStruct(sky_image.shape, f32),
            ),
            in_specs=[vmem, anywhere, anywhere, anywhere],
            out_specs=(anywhere, vmem),
            scratch_shapes=[
                pltpu.VMEM((n_basis, 2 * tile, width), f32),
                pltpu.VMEM((bases, 2, 2 * tile, tile), f32),
                pltpu.VMEM((LEVELS - 1, 2, tile, tile), f32),
                pltpu.VMEM((bases, 2 * used, 2 * tile), bf16),
                pltpu.VMEM((4 * tile, bases * 2 * tile), bf16),
                pltpu.VMEM((bases, LEVELS, 2 * tile, 2 * tile), bf16),
                pltpu.VMEM((bases, LEVELS, 2 * tile, 2 * tile), bf16),
                pltpu.VMEM((bases, tiles, tile, tile), f32),
                pltpu.VMEM((bases, tiles, tile, tile), f32),
                pltpu.VMEM((bases, tiles, used, tile), bf16),
                pltpu.VMEM((bases, tiles, used, tile), bf16),
                pltpu.VMEM((tiles, tile, tile), f32),
                pltpu.VMEM((bases, tiles, tile, tile), f32),
                pltpu.VMEM((tiles, bases * 2 * tile, tile), bf16),
                pltpu.VMEM((tiles, bases * 2 * tile, tile), bf16),
                pltpu.VMEM((n_basis, 2 * tile, width), f32),
                pltpu.VMEM((n_basis, halo, width), f32),
                pltpu.VMEM((n_basis, tile, width), f32),
                dma((1 + 2 * tiles,)),
                dma((bases * tiles,)),
            ] + [dma((n_basis,)) for _ in range(8)],
            compiler_params=pltpu.CompilerParams(
                collective_id=0, has_side_effects=True, vmem_limit_bytes=48 * 2**20
            ),
        )(sky_image, table, dual_coeffs, thresholds)

    placed = (P("strip", "basis"), P("basis", "strip", None), P("basis", "strip", None))
    return jax.shard_map(
        on_device,
        mesh=mesh,
        in_specs=placed,
        out_specs=(P("basis", "strip", None), P("strip", "basis")),
        check_vma=False,
    )
```

profile of v0, /device:TPU:0, one launch (start us, length us, event | category | flops | bytes accessed | tf_op | source)
XLA Modules:
  0.0 38.3 jit_solution(18146368474985009026)
XLA Ops:
  0.6 0.0 copy-start
  0.6 1.6 %copy-done = f32[8,2,256,128]{3,2,1,0:T(8,128)S(1)} copy-done((f32[8,2,256,128]{3,2,1,0:T(8,128)S(1)}, f32[8,2,256,128]{3,2,1,0:T(8,128)}, u32[]{:S(2)}) %copy-start) | copy-done | bytes 2097176
  2.2 0.0 copy-start.1
  2.2 1.2 %copy-done.1 = f32[2,128,1024]{2,1,0:T(8,128)S(1)} copy-done((f32[2,128,1024]{2,1,0:T(8,128)S(1)}, f32[2,128,1024]{2,1,0:T(8,128)}, u32[]{:S(2)}) %copy-start.1) | copy-done | bytes 1048600
  3.5 0.0 copy-start.2
  3.5 1.2 %copy-done.2 = f32[2,128,1024]{2,1,0:T(8,128)S(1)} copy-done((f32[2,128,1024]{2,1,0:T(8,128)S(1)}, f32[2,128,1024]{2,1,0:T(8,128)}, u32[]{:S(2)}) %copy-start.2) | copy-done | bytes 1048600
  4.7 0.0 copy-start.3
  4.7 0.9 %copy-done.3 = f32[128,256]{1,0:T(8,128)S(1)} copy-done((f32[128,256]{1,0:T(8,128)S(1)}, f32[128,256]{1,0:T(8,128)}, u32[]{:S(2)}) %copy-start.3) | copy-done | bytes 131096
  5.6 31.1 %shard_map.59 = (f32[2,128,1024]{2,1,0:T(8,128)S(1)}, f32[128,256]{1,0:T(8,128)S(1)}) custom-call(f32[128,256]{1,0:T(8,128)S(1)} %copy-done.3, f32[8,2,256,128]{3,2,1,0:T(8,128)S(1)} %copy-done, f32[2,128,1024]{2,1,0:T(8,128)S(1)} %copy-done.1, f32[2,128,1024]{2,1,0:T(8,128)S(1)} %copy-done.2), custom_call_target="tpu_custom_call" | custom-call | tf_op jit(solution)/shard_map/pallas_call | solution.py:390
  36.7 1.0 %copy.8 = f32[2,128,1024]{2,1,0:T(8,128)} copy(f32[2,128,1024]{2,1,0:T(8,128)S(1)} %get-tuple-element.4) | data formatting | bytes 2097152
  37.6 0.7 %copy.9 = f32[128,256]{1,0:T(8,128)} copy(f32[128,256]{1,0:T(8,128)S(1)} %get-tuple-element.5) | data formatting | bytes 262144
Async XLA Ops:
  0.6 1.6 %copy-start = (f32[8,2,256,128]{3,2,1,0:T(8,128)S(1)}, f32[8,2,256,128]{3,2,1,0:T(8,128)}, u32[]{:S(2)}) copy-start(f32[8,2,256,128]{3,2,1,0:T(8,128)} %constant.2.clone.table) | copy-start | bytes 6291460
  2.2 1.2 %copy-start.1 = (f32[2,128,1024]{2,1,0:T(8,128)S(1)}, f32[2,128,1024]{2,1,0:T(8,128)}, u32[]{:S(2)}) copy-start(f32[2,128,1024]{2,1,0:T(8,128)} %dual.1) | copy-start | bytes 3145732
  3.5 1.2 %copy-start.2 = (f32[2,128,1024]{2,1,0:T(8,128)S(1)}, f32[2,128,1024]{2,1,0:T(8,128)}, u32[]{:S(2)}) copy-start(f32[2,128,1024]{2,1,0:T(8,128)} %thresholds.1) | copy-start | bytes 3145732
  4.7 0.9 %copy-start.3 = (f32[128,256]{1,0:T(8,128)S(1)}, f32[128,256]{1,0:T(8,128)}, u32[]{:S(2)}) copy-start(f32[128,256]{1,0:T(8,128)} %sky.1) | copy-start | bytes 393220
where the time goes:
time: 38.5 us; the launch traced here: 38.3 us
  Pallas kernels  31.1 us (81%)
  local copies, waits for them, and re-layouts  6.57 us (17%)
  between operations  0.65 us (2%)
    pallas_call x1, Pallas kernels, on_device(): pl.pallas_call(functools.partial(kernel, (n_strip, n_basis, bases, tile,...  31.1 us
    unnamed x10, local copies, waits for them, and re-layouts  6.57 us

commit v1 on v0

--- a/solution.py
+++ b/solution.py
@@ -198,26 +198,37 @@
             device_id=target, device_id_type=pl.DeviceIdType.MESH,
         )
 
-    block_copies = [None]
+    halves = ((0, tile // 2), (tile // 2, tile // 2))
+    halo_halves = [(first, min(count, halo - first)) for first, count in halves if halo > first]
+    block_copies, halo_copies = {}, {}
+    single = list(range(1, n_basis))
     for d in range(1, n_basis):
-        block_copies.append(
-            remote(sky, xg.at[me, pl.ds(0, tile)], bs_send.at[d], bs_recv.at[d], (strip, peers[d]))
-        )
-    halo_copies = [
-        remote(sky.at[pl.ds(0, halo)], xg.at[me, pl.ds(tile, halo)], hs_send.at[0], hs_recv.at[0], (behind, me))
-    ]
-    for d in range(1, n_basis):
-        halo_copies.append(
-            remote(
-                xg.at[peers[d], pl.ds(0, halo)], xg.at[peers[d], pl.ds(tile, halo)],
-                hs_send.at[d], hs_recv.at[d], (behind, me),
-            )
-        )
-    halo_copies[0].start()
-    for d in range(1, n_basis):
-        block_copies[d].start()
-
-    xg[me, 0:tile, :] = sky[...]
+        for p, (first, count) in enumerate(halves):
+            rows = pl.ds(first, count)
+            if d in single:
+                source, held, target = sky.at[rows], me, peers[d]
+            else:
+                bit = (d & -d) if p == 0 else 1 << (d.bit_length() - 1)
+                held, target = peers[d ^ bit], peers[bit]
+                source = xg.at[held, rows]
+            block_copies[d, p] = remote(
+                source, xg.at[held, rows], bs_send.at[d, p], bs_recv.at[d, p], (strip, target)
+            )
+    for d in range(n_basis):
+        for p, (first, count) in enumerate(halo_halves):
+            source = sky.at[pl.ds(first, count)] if d == 0 else xg.at[peers[d], pl.ds(first, count)]
+            halo_copies[d, p] = remote(
+                source, xg.at[peers[d], pl.ds(tile + first, count)],
+                hs_send.at[d, p], hs_recv.at[d, p], (behind, me),
+            )
+    for p in range(2):
+        for d in single:
+            block_copies[d, 1 - p if d == 1 else p].start()
+    for p in range(len(halo_halves)):
+        halo_copies[0, p].start()
+    own_copy = pltpu.make_async_copy(sky, xg.at[me, pl.ds(0, tile)], load_sem.at[1 + 2 * tiles])
+    own_copy.start()
+
     if halo < tile:
         for d in range(n_basis):
             xg[d, tile + halo :, :] = jnp.zeros((tile - halo, width), jnp.float32)
@@ -247,12 +258,21 @@
                 g_an[b, level, s : s + tile, :tile] = g_high
                 g_an[b, level, s : s + tile, tile:] = g_low
 
-    for d in range(1, n_basis):
-        block_copies[d].wait_recv()
-        halo_copies[d].start()
+    own_copy.wait()
+    arrivals = [(d, 1 - p if d == 1 else p) for p in range(2) for d in single]
+    arrivals += [(d, p) for d in range(1, n_basis) if d not in single for p in range(2)]
+    for d, p in arrivals:
+        block_copies[d, p].wait_recv()
+        for other in range(d + 1, n_basis):
+            bit = (other & -other) if p == 0 else 1 << (other.bit_length() - 1)
+            if other not in single and other ^ bit == d:
+                block_copies[other, p].start()
+        if (d, p) in halo_copies:
+            halo_copies[d, p].start()
 
     for d in range(n_basis):
-        halo_copies[d].wait_recv()
+        for p in range(len(halo_halves)):
+            halo_copies[d, p].wait_recv()
         x_high, x_low = bf16_pair(xg[peers[d]])
         for b in range(bases):
             wide = dot(a_lhs[b], x_high)
@@ -342,31 +362,35 @@
         e_l = jnp.concatenate([e_lo[at * per_block + part] for part in range(per_block)], axis=1)
         wide = dot(a_t[...], e_h)
         pbuf[d, :, :] = wide[: 2 * tile] + wide[2 * tile :] + dot(a_t[: 2 * tile], e_l)
-        carry_copies[d] = remote(
-            pbuf.at[d, pl.ds(tile, halo)], hbuf.at[d], ps_send.at[d], ps_recv.at[d], (after, me)
-        )
-        carry_copies[d].start()
+        for p, (first, count) in enumerate(halo_halves):
+            carry_copies[d, p] = remote(
+                pbuf.at[d, pl.ds(tile + first, count)], hbuf.at[d, pl.ds(first, count)],
+                ps_send.at[d, p], ps_recv.at[d, p], (after, me),
+            )
+            carry_copies[d, p].start()
     for d in order:
-        carry_copies[d].wait_recv()
-        pbuf[d, :halo, :] = pbuf[d, :halo, :] + hbuf[d]
-        if d > 0:
-            part_copies[d] = remote(
-                pbuf.at[d, pl.ds(0, tile)], rbuf.at[d], rs_send.at[d], rs_recv.at[d], (strip, peers[d])
-            )
-            part_copies[d].start()
+        for p, (first, count) in enumerate(halves):
+            if (d, p) in carry_copies:
+                rows = pl.ds(*halo_halves[p])
+                carry_copies[d, p].wait_recv()
+                pbuf[d, rows, :] = pbuf[d, rows, :] + hbuf[d, rows, :]
+            if d > 0:
+                part_copies[d, p] = remote(
+                    pbuf.at[d, pl.ds(first, count)], rbuf.at[d, pl.ds(first, count)],
+                    rs_send.at[d, p], rs_recv.at[d, p], (strip, peers[d]),
+                )
+                part_copies[d, p].start()
     total = pbuf[0, :tile, :]
     for d in order:
         if d > 0:
-            part_copies[d].wait_recv()
+            for p in range(len(halves)):
+                part_copies[d, p].wait_recv()
             total = total + rbuf[d]
     out_image[...] = total * norm_scale
 
-    for d in range(n_basis):
-        halo_copies[d].wait_send()
-        carry_copies[d].wait_send()
-        if d > 0:
-            block_copies[d].wait_send()
-            part_copies[d].wait_send()
+    sent = (block_copies, halo_copies, carry_copies, part_copies)
+    for copy in [copy for group in sent for copy in group.values()]:
+        copy.wait_send()
     for copy in stores:
         copy.wait()
 
@@ -393,7 +417,7 @@
                 jax.ShapeDtypeStruct(dual_coeffs.shape, f32),
                 jax.ShapeDtypeStruct(sky_image.shape, f32),
             ),
-            in_specs=[vmem, anywhere, anywhere, anywhere],
+            in_specs=[anywhere, anywhere, anywhere, anywhere],
             out_specs=(anywhere, vmem),
             scratch_shapes=[
                 pltpu.VMEM((n_basis, 2 * tile, width), f32),
@@ -414,11 +438,11 @@
                 pltpu.VMEM((n_basis, 2 * tile, width), f32),
                 pltpu.VMEM((n_basis, halo, width), f32),
                 pltpu.VMEM((n_basis, tile, width), f32),
-                dma((1 + 2 * tiles,)),
+                dma((2 + 2 * tiles,)),
                 dma((bases * tiles,)),
-            ] + [dma((n_basis,)) for _ in range(8)],
+            ] + [dma((n_basis, 2)) for _ in range(8)],
             compiler_params=pltpu.CompilerParams(
-                collective_id=0, has_side_effects=True, vmem_limit_bytes=48 * 2**20
+                collective_id=0, has_side_effects=True, vmem_limit_bytes=67_043_328 - 1_400_000
             ),
         )(sky_image, table, dual_coeffs, thresholds)
 

time: 38.5 us -> 34.7 us (0.901)
  local copies, waits for them, and re-layouts: 6.57 us -> 3 us
    unnamed x10 -> x4, local copies, waits for them, and re-layouts: 6.57 us -> 3 us
where the time goes in v1:
time: 34.7 us; the launch traced here: 34.6 us
  Pallas kernels  30.9 us (89%)
  local copies, waits for them, and re-layouts  3 us (9%)
  between operations  0.65 us (2%)
    pallas_call x1, Pallas kernels, on_device(): pl.pallas_call(functools.partial(kernel, (n_strip, n_basis, bases, tile,...  30.9 us
    unnamed x4, local copies, waits for them, and re-layouts  3 us

profile of v1, /device:TPU:0, one launch (start us, length us, event | category | flops | bytes accessed | tf_op | source)
XLA Modules:
  0.0 34.6 jit_solution(8793763017288246076)
XLA Ops:
  0.6 30.9 %shard_map.59 = (f32[2,128,1024]{2,1,0:T(8,128)}, f32[128,256]{1,0:T(8,128)}) custom-call(f32[128,256]{1,0:T(8,128)} %sky.1, f32[8,2,256,128]{3,2,1,0:T(8,128)} %constant.2.clone.table, f32[2,128,1024]{2,1,0:T(8,128)} %dual.1, f32[2,128,1024]{2,1,0:T(8,128)} %thresholds.1), custom_call_target="tpu_custom_call" | custom-call | tf_op jit(solution)/shard_map/pallas_call | solution.py:414
  31.6 0.0 copy-start
  31.6 2.3 %copy.8 = f32[2,128,1024]{2,1,0:T(8,128)} copy(f32[2,128,1024]{2,1,0:T(8,128)} %get-tuple-element.4) | data formatting | bytes 2097152
  33.9 0.0 copy-done
  33.9 0.7 %copy.9 = f32[128,256]{1,0:T(8,128)} copy(f32[128,256]{1,0:T(8,128)S(1)} %copy-done) | data formatting | bytes 262144
Async XLA Ops:
  31.6 2.4 %copy-start = (f32[128,256]{1,0:T(8,128)S(1)}, f32[128,256]{1,0:T(8,128)}, u32[]{:S(2)}) copy-start(f32[128,256]{1,0:T(8,128)} %get-tuple-element.5) | copy-start | bytes 393220
